TPU v7x, 512 devices: a whole 4x4x16 slice. The times are simulated.
512 devices in a mesh: rows: 64 (over x, z_lo, core), cols: 8 (over y, z_hi).
Axes of the slice: x: 4, y: 4, z: 16 (z_hi: 2, z_lo: 8; z = z_hi * 8 + z_lo), core: 2. Of those that a mesh axis runs over, the one named last changes fastest.
Arguments:
- features: bfloat16 [786432, 256], P(('rows', 'cols')), may hold values from -6 to 6
- adj_values: bfloat16 [6144, 3, 128, 128], P(('rows', 'cols')), may hold values from -0.3125 to 0.3125
- adj_offset: int32 [6144, 3], P(('rows', 'cols')), may hold values from -2 to 2, as said below
- adj_count: int32 [6144], P(('rows', 'cols')), may hold values from 1 to 3, as said below
- weight: bfloat16 [256, 256], replicated, may hold values from -0.375 to 0.375
- bias_vector: float32 [256], replicated, may hold values from -4 to 4
- cotangent: bfloat16 [786432, 256], P(('rows', 'cols')), may hold values from -6 to 6
Outputs:
- activated: bfloat16 [786432, 256], P(('rows', 'cols'))
- grad_features: bfloat16 [786432, 256], P(('rows', 'cols'))
- grad_weight: float32 [256, 256], replicated
- grad_bias: float32 [256], replicated
Inputs may be any that keep to these rules, and one draw needn't show every extreme that they name: Slot 0 of every row block has offset 0; the offsets of one row block are distinct, and for row block i every i + adj_offset[i, s] lies in 0 to 6143. Row block i uses its slots 0 to adj_count[i] - 1; the values and offsets of its other slots are ignored. In every draw all row blocks of one device, drawn from the seed, use all 3 slots.
All inputs are finite; a program needn't handle non-finite values.
Results may differ from a plain program's by a relative error of at most 0.0075.
Values may be sent and summed in bfloat16 or wider, within the bound.
A program may use at most 64 MiB of HBM per device.

v0:
```python
import math
import jax
import jax.numpy as jnp
from jax import lax
from jax.sharding import PartitionSpec as P

BAND = 2


def shifted(value, axis, steps):
    count = lax.axis_size(axis)
    pairs = [(source, (source + steps) % count) for source in range(count)]
    return lax.ppermute(value, axis, pairs)


def from_behind(value, axis, steps):
    count = lax.axis_size(axis)
    initial, last = (max(0, -steps), min(count, count - steps))
    return lax.ppermute(value, axis, [(source, source + steps) for source in range(initial, last)])


def fetch_lower(rim_piece):
    narrow_step = shifted(rim_piece, "cols", 1)
    wide_step = from_behind(narrow_step, "rows", 1)
    return jnp.where(lax.axis_index("cols") == 0, wide_step, narrow_step)


def fetch_upper(rim_piece):
    narrow_step = shifted(rim_piece, "cols", -1)
    wide_step = from_behind(narrow_step, "rows", -1)
    return jnp.where(lax.axis_index("cols") == lax.axis_size("cols") - 1, wide_step, narrow_step)


def spill_lower(rim_piece):
    narrow_step = shifted(rim_piece, "cols", 1)
    wide_step = from_behind(narrow_step, "rows", 1)
    return jnp.where(lax.axis_index("cols") == 0, wide_step, narrow_step)


def spill_upper(rim_piece):
    narrow_step = shifted(rim_piece, "cols", -1)
    wide_step = from_behind(narrow_step, "rows", -1)
    return jnp.where(lax.axis_index("cols") == lax.axis_size("cols") - 1, wide_step, narrow_step)


def on_device(features, adj_values, adj_offset, adj_count, weight, bias_vector, cotangent):
    blocks = adj_offset.shape[0]
    slot_total = adj_offset.shape[1]
    block_rows = adj_values.shape[2]
    feat_width = features.shape[1]
    band_reach = BAND
    span_blocks = blocks + 2 * band_reach
    rim_rows = band_reach * block_rows
    slot_index = lax.broadcasted_iota(jnp.int32, (blocks, slot_total), 1)
    block_index = lax.broadcasted_iota(jnp.int32, (blocks, slot_total), 0)
    active = slot_index < adj_count[:, None]
    target = block_index + band_reach + adj_offset
    from_below = fetch_lower(features[features.shape[0] - rim_rows :])
    from_above = fetch_upper(features[:rim_rows])
    extended = jnp.concatenate([from_below, features, from_above], 0)
    window = extended.reshape(span_blocks, block_rows, feat_width)
    picked = window[target]
    picked = jnp.where(active[:, :, None, None], picked, jnp.zeros_like(picked))
    summed = jnp.einsum("bsac,bscf->baf", adj_values, picked, preferred_element_type=jnp.float32)
    aggregated = summed.reshape(-1, feat_width).astype(jnp.bfloat16)
    preact = jnp.dot(aggregated, weight, preferred_element_type=jnp.float32) + bias_vector
    activated = jax.nn.silu(preact).astype(jnp.bfloat16)
    sigmoid_pre = jax.nn.sigmoid(preact)
    grad_pre = (
        cotangent.astype(jnp.float32) * sigmoid_pre * (1.0 + preact * (1.0 - sigmoid_pre))
    ).astype(jnp.bfloat16)
    partial_weight = lax.dot_general(
        aggregated, grad_pre, (((0,), (0,)), ((), ())), preferred_element_type=jnp.float32
    )
    partial_bias = jnp.sum(grad_pre.astype(jnp.float32), axis=0)
    total_weight, total_bias = lax.psum((partial_weight, partial_bias), ("rows", "cols"))
    nodes_total = features.shape[0] * lax.axis_size("rows") * lax.axis_size("cols")
    norm_scale = 1.0 / math.sqrt(nodes_total)
    grad_weight = total_weight * norm_scale
    grad_bias = total_bias * norm_scale
    upstream = lax.dot_general(
        grad_pre, weight, (((1,), (1,)), ((), ())), preferred_element_type=jnp.float32
    ).astype(jnp.bfloat16)
    slot_terms = jnp.einsum(
        "bsac,baf->bscf",
        adj_values,
        upstream.reshape(blocks, block_rows, feat_width),
        preferred_element_type=jnp.float32,
    )
    slot_terms = jnp.where(active[:, :, None, None], slot_terms, jnp.zeros_like(slot_terms))
    empty = jnp.zeros((span_blocks, block_rows, feat_width), jnp.float32)
    spread = empty.at[target.reshape(-1)].add(slot_terms.reshape(-1, block_rows, feat_width))
    lower_part = spread[:band_reach]
    middle = spread[band_reach : band_reach + blocks]
    upper_part = spread[band_reach + blocks :]
    from_above_dev = spill_upper(lower_part)
    from_below_dev = spill_lower(upper_part)
    combined = middle.at[:band_reach].add(from_below_dev)
    combined = combined.at[blocks - band_reach :].add(from_above_dev)
    grad_features = combined.reshape(-1, feat_width).astype(jnp.bfloat16)
    return (activated, grad_features, grad_weight, grad_bias)


def solution(mesh):
    return jax.shard_map(
        on_device,
        mesh=mesh,
        in_specs=(
            P(("rows", "cols"), None),
            P(("rows", "cols"), None, None, None),
            P(("rows", "cols"), None),
            P(("rows", "cols")),
            P(),
            P(),
            P(("rows", "cols"), None),
        ),
        out_specs=(P(("rows", "cols"), None), P(("rows", "cols"), None), P(), P()),
        check_vma=False,
    )
```

profile of v0, /device:TPU:4, one launch (start us, length us, event | category | flops | bytes accessed | tf_op | source)
XLA Modules:
  0.0 578.7 jit_solution(4762388384572714263)
XLA Ops:
  7.2 0.0 copy-start
  7.2 0.0 all-reduce.2.cloned.1.call-start
  7.2 1.1 fusion.11
  8.4 15.7 %collective-permute-start = (bf16[256,256]{1,0:T(8,128)(2,1)S(1)}, bf16[256,256]{1,0:T(8,128)(2,1)S(1)}, u32[]{:S(2)}, u32[]{:S(2)}) collective-permute-start(bf16[256,256]{1,0:T(8,128)(2,1)S(1)} %get-tuple-element.35), channel_id=1, source_target_pairs={{0,1},{1,2},{2,3},{3,4},{4,5},{5,6},{6,7},{7,0},{8,9},{9,10},{10,1... | collective-permute-start | bytes 393224 | tf_op jit(solution)/shard_map/ppermute | solution.py:13
  24.1 4.4 collective-permute-start.2
  28.5 0.7 compare_select_fusion
  29.2 0.1 copy.15
  29.3 0.1 reshape.133
  29.3 0.7 iota_compare_fusion
  30.1 0.2 collective-permute-done
  30.3 1.9 collective-permute-start.1
  32.3 0.1 copy.14
  32.3 0.1 reshape.138
  32.4 19.6 %collective-permute-done.2 = bf16[256,256]{1,0:T(8,128)(2,1)S(1)} collective-permute-done((bf16[256,256]{1,0:T(8,128)(2,1)S(1)}, bf16[256,256]{1,0:T(8,128)(2,1)S(1)}, u32[]{:S(2)}, u32[]{:S(2)}) %collective-permute-start.2) | collective-permute-done | bytes 131104 | tf_op jit(solution)/shard_map/ppermute | solution.py:13
  52.0 1.9 collective-permute-start.3
  54.0 0.0 collective-permute-done.1
  54.0 2.5 collective-permute-done.3
  56.5 0.1 pad_maximum_fusion
  56.6 2.3 gather_fusion
  58.9 2.4 bitcast_convert_fusion
  61.3 0.0 copy-start.6
  61.3 1.8 convert_reduce_fusion
  63.1 0.0 copy-done.6
  63.1 0.9 copy-done.2
  64.0 0.4 convolution_convert_fusion
  64.4 3.1 broadcast_select_fusion
  67.5 6.1 %copy.17 = f32[36,128,256]{2,1,0:T(8,128)} copy(f32[36,128,256]{1,2,0:T(8,128)} %bitcast.28) | data formatting | bytes 9437184 | tf_op jit(solution)/shard_map/reshape | solution.py:92
  73.7 0.2 broadcast_in_dim.36
  73.9 8.9 %scatter_fusion = f32[16,128,256]{2,1,0:T(8,128)S(1)} fusion(f32[16,128,256]{2,1,0:T(8,128)S(1)} %broadcast_in_dim.36, s32[36]{0:T(128)S(1)} %fusion.8, f32[36,128,256]{2,1,0:T(8,128)} %copy.17), kind=kCustom, calls=%fused_computation.1 | custom fusion | flops 1179648 | bytes 14155920 | tf_op jit(solution)/shard_map/scatter-add | solution.py:92
  82.7 0.8 fusion.10
  83.6 8.7 %collective-permute-start.4 = (f32[2,128,256]{2,1,0:T(8,128)}, f32[2,128,256]{2,1,0:T(8,128)}, u32[]{:S(2)}, u32[]{:S(2)}) collective-permute-start(f32[2,128,256]{2,1,0:T(8,128)} %get-tuple-element.33), channel_id=1, source_target_pairs={{0,1},{1,2},{2,3},{3,4},{4,5},{5,6},{6,7},{7,0},{8,9},{9,10},{10,1... | collective-permute-start | bytes 786440 | tf_op jit(solution)/shard_map/ppermute | solution.py:13
  92.3 7.9 %collective-permute-start.6 = (f32[2,128,256]{2,1,0:T(8,128)}, f32[2,128,256]{2,1,0:T(8,128)S(1)}, u32[]{:S(2)}, u32[]{:S(2)}) collective-permute-start(f32[2,128,256]{2,1,0:T(8,128)} %get-tuple-element.32), channel_id=1, source_target_pairs={{0,7},{1,0},{2,1},{3,2},{4,3},{5,4},{6,5},{7,6},{8,15},{9,8},{10,9... | collective-permute-start | bytes 786440 | tf_op jit(solution)/shard_map/ppermute | solution.py:13
  100.2 2.5 fusion.12
  102.7 0.0 all-reduce.2.cloned.1.call-update
  102.8 108.2 %psum.15 = f32[256]{0:T(256)S(1)} all-reduce(f32[256]{0:T(256)S(1)} %get-tuple-element.28), channel_id=1, replica_groups=mesh['rows'=64,'cols'=8] {'rows','cols'}, use_global_device_ids=true, to_apply=%region_3.4 | all-reduce | flops 256 | bytes 2048 | tf_op jit(solution)/shard_map/psum | solution.py:76
  210.9 0.0 collective-permute-done.4
  210.9 1.9 collective-permute-start.5
  212.8 0.6 broadcast_multiply_fusion.1
  213.4 1.3 slice.73
  214.7 0.0 collective-permute-done.6
  214.7 11.1 %collective-permute-start.7 = (f32[2,128,256]{2,1,0:T(8,128)S(1)}, f32[2,128,256]{2,1,0:T(8,128)}, u32[]{:S(2)}, u32[]{:S(2)}) collective-permute-start(f32[2,128,256]{2,1,0:T(8,128)S(1)} %collective-permute-done.6), channel_id=1, source_target_pairs={{8,0},{16,8},{24,16},{32,24},{40,32},{48,40},{56,48},{64,56},{72,6... | collective-permute-start | bytes 786440 | tf_op jit(solution)/shard_map/ppermute | solution.py:19
  225.9 338.5 %all-reduce.2.cloned.1.call-done = f32[256,256]{1,0:T(8,128)} async-done(((f32[256,256]{1,0:T(8,128)}), f32[256,256]{1,0:T(8,128)}) %all-reduce.2.cloned.1.call-update) | async-done | bytes 262160 | tf_op jit(solution)/shard_map/psum | solution.py:76
  564.3 1.7 broadcast_multiply_fusion
  566.0 0.0 collective-permute-done.5
  566.0 1.7 fusion.7
  567.7 0.0 collective-permute-done.7
  567.7 1.7 fusion.6
  569.5 2.4 convert_element_type.37
  (15 shorter events, 0.1 us)
Async XLA Ops:
  7.2 51.7 %copy-start = (bf16[12,3,128,128]{3,2,1,0:T(8,128)(2,1)S(1)}, bf16[12,3,128,128]{3,2,1,0:T(8,128)(2,1)}, u32[]{:S(2)}) copy-start(bf16[12,3,128,128]{3,2,1,0:T(8,128)(2,1)} %param.12) | copy-start | bytes 3538948
  7.2 49.3 %copy-start.1 = (bf16[1536,256]{1,0:T(8,128)(2,1)S(1)}, bf16[1536,256]{1,0:T(8,128)(2,1)}, u32[]{:S(2)}) copy-start(bf16[1536,256]{1,0:T(8,128)(2,1)} %param.11) | copy-start | bytes 2359300
  7.2 557.1 %all-reduce.2.cloned.1.call-start = ((), (), s32[]{:S(2)}) async-start(), calls=%async_computation | async-start | bytes 524288 | tf_op jit(solution)/shard_map/psum | solution.py:76
  8.4 22.0 %collective-permute-start = (bf16[256,256]{1,0:T(8,128)(2,1)S(1)}, bf16[256,256]{1,0:T(8,128)(2,1)S(1)}, u32[]{:S(2)}, u32[]{:S(2)}) collective-permute-start(bf16[256,256]{1,0:T(8,128)(2,1)S(1)} %get-tuple-element.35), channel_id=1, source_target_pairs={{0,1},{1,2},{2,3},{3,4},{4,5},{5,6},{6,7},{7,0},{8,9},{9,10},{10,1... | collective-permute-start | bytes 393224 | tf_op jit(solution)/shard_map/ppermute | solution.py:13
  24.1 28.0 %collective-permute-start.2 = (bf16[256,256]{1,0:T(8,128)(2,1)S(1)}, bf16[256,256]{1,0:T(8,128)(2,1)S(1)}, u32[]{:S(2)}, u32[]{:S(2)}) collective-permute-start(bf16[256,256]{1,0:T(8,128)(2,1)S(1)} %get-tuple-element.36), channel_id=1, source_target_pairs={{0,7},{1,0},{2,1},{3,2},{4,3},{5,4},{6,5},{7,6},{8,15},{9,8},{10,9... | collective-permute-start | bytes 393224 | tf_op jit(solution)/shard_map/ppermute | solution.py:13
  30.3 23.7 %collective-permute-start.1 = (bf16[256,256]{1,0:T(8,128)(2,1)S(1)}, bf16[256,256]{1,0:T(8,128)(2,1)S(1)}, u32[]{:S(2)}, u32[]{:S(2)}) collective-permute-start(bf16[256,256]{1,0:T(8,128)(2,1)S(1)} %collective-permute-done), channel_id=1, source_target_pairs={{0,8},{8,16},{16,24},{24,32},{32,40},{40,48},{48,56},{56,64},{64,7... | collective-permute-start | bytes 393224 | tf_op jit(solution)/shard_map/ppermute | solution.py:19
  52.0 4.4 collective-permute-start.3
  58.9 2.4 copy-start.3
  58.9 2.4 copy-start.4
  58.9 2.5 copy-start.5
  61.3 1.9 copy-start.6
  63.1 0.9 copy-start.2
  83.6 127.3 %collective-permute-start.4 = (f32[2,128,256]{2,1,0:T(8,128)}, f32[2,128,256]{2,1,0:T(8,128)}, u32[]{:S(2)}, u32[]{:S(2)}) collective-permute-start(f32[2,128,256]{2,1,0:T(8,128)} %get-tuple-element.33), channel_id=1, source_target_pairs={{0,1},{1,2},{2,3},{3,4},{4,5},{5,6},{6,7},{7,0},{8,9},{9,10},{10,1... | collective-permute-start | bytes 786440 | tf_op jit(solution)/shard_map/ppermute | solution.py:13
  92.3 122.4 %collective-permute-start.6 = (f32[2,128,256]{2,1,0:T(8,128)}, f32[2,128,256]{2,1,0:T(8,128)S(1)}, u32[]{:S(2)}, u32[]{:S(2)}) collective-permute-start(f32[2,128,256]{2,1,0:T(8,128)} %get-tuple-element.32), channel_id=1, source_target_pairs={{0,7},{1,0},{2,1},{3,2},{4,3},{5,4},{6,5},{7,6},{8,15},{9,8},{10,9... | collective-permute-start | bytes 786440 | tf_op jit(solution)/shard_map/ppermute | solution.py:13
  210.9 355.1 %collective-permute-start.5 = (f32[2,128,256]{2,1,0:T(8,128)}, f32[2,128,256]{2,1,0:T(8,128)}, u32[]{:S(2)}, u32[]{:S(2)}) collective-permute-start(f32[2,128,256]{2,1,0:T(8,128)} %collective-permute-done.4), channel_id=1, source_target_pairs={{0,8},{8,16},{16,24},{24,32},{32,40},{40,48},{48,56},{56,64},{64,7... | collective-permute-start | bytes 786440 | tf_op jit(solution)/shard_map/ppermute | solution.py:19
  214.7 353.0 %collective-permute-start.7 = (f32[2,128,256]{2,1,0:T(8,128)S(1)}, f32[2,128,256]{2,1,0:T(8,128)}, u32[]{:S(2)}, u32[]{:S(2)}) collective-permute-start(f32[2,128,256]{2,1,0:T(8,128)S(1)} %collective-permute-done.6), channel_id=1, source_target_pairs={{8,0},{16,8},{24,16},{32,24},{40,32},{48,40},{56,48},{64,56},{72,6... | collective-permute-start | bytes 786440 | tf_op jit(solution)/shard_map/ppermute | solution.py:19
Sparse Core Ops, SparseCore 0:
  102.9 461.4 all-reduce.1
where the time goes:
time: 579 us
  waiting for transfers between devices  361 us (62%)
  blocking collectives  108 us (19%)
  starting transfers between devices  53.7 us (9%)
  other arithmetic  18.4 us (3%)
  between operations  14.3 us (2%)
  local copies, waits for them, and re-layouts  13.2 us (2%)
  matrix products  10.2 us (2%)
    psum x1, waiting for transfers between devices, on_device(): lax.psum((partial_weight, partial_bias), ('rows', 'cols'))  338 us
    psum x1, blocking collectives, on_device(): lax.psum((partial_weight, partial_bias), ('rows', 'cols'))  108 us
    ppermute x4, starting transfers between devices, shifted(): return lax.ppermute(value, axis, pairs)  36.7 us
    ppermute x4, waiting for transfers between devices, shifted(): return lax.ppermute(value, axis, pairs)  19.8 us
    ppermute x4, starting transfers between devices, from_behind(): lax.ppermute(value, axis, [(source, source + steps) for source in range(i...  16.9 us
  transfers between devices with their start and end apart: 9, of which 4 were waited for; matrix products, arithmetic and copies ran while one was open for 2% of the time, Pallas kernels for 0%

commit v1 on v0

--- a/solution.py
+++ b/solution.py
@@ -73,7 +73,7 @@
         aggregated, grad_pre, (((0,), (0,)), ((), ())), preferred_element_type=jnp.float32
     )
     partial_bias = jnp.sum(grad_pre.astype(jnp.float32), axis=0)
-    total_weight, total_bias = lax.psum((partial_weight, partial_bias), ("rows", "cols"))
+    total_weight, total_bias = lax.psum(lax.psum((partial_weight, partial_bias), "rows"), "cols")
     nodes_total = features.shape[0] * lax.axis_size("rows") * lax.axis_size("cols")
     norm_scale = 1.0 / math.sqrt(nodes_total)
     grad_weight = total_weight * norm_scale

time: 579 us -> 1060 us (1.83)
  the two profiles are of different devices: /device:TPU:4 before, /device:TPU:2 now
where the time goes in v1:
time: 1060 us
  waiting for transfers between devices  712 us (67%)
  blocking collectives  243 us (23%)
  starting transfers between devices  44.5 us (4%)
  other arithmetic  18.4 us (2%)
  between operations  14.3 us (1%)
  local copies, waits for them, and re-layouts  13.1 us (1%)
    psum x1, waiting for transfers between devices, on_device(): lax.psum((partial_weight, partial_bias), 'rows')  478 us
    psum x1, blocking collectives, on_device(): lax.psum((partial_weight, partial_bias), 'rows')  200 us
    psum x1, waiting for transfers between devices, on_device(): lax.psum(lax.psum((partial_weight, partial_bias), 'rows'), 'cols')  184 us
    ppermute x4, waiting for transfers between devices, shifted(): return lax.ppermute(value, axis, pairs)  48 us
    psum x1, blocking collectives, on_device(): lax.psum(lax.psum((partial_weight, partial_bias), 'rows'), 'cols')  42.3 us
    ppermute x4, starting transfers between devices, shifted(): return lax.ppermute(value, axis, pairs)  36.7 us
  transfers between devices with their start and end apart: 10, of which 6 were waited for; matrix products, arithmetic and copies ran while one was open for 1% of the time, Pallas kernels for 0%

profile of v1, /device:TPU:2, one launch (start us, length us, event | category | flops | bytes accessed | tf_op | source)
XLA Modules:
  0.0 1055.0 jit_solution(18281853844139140296)
XLA Ops:
  7.2 0.0 copy-start
  7.2 0.0 all-reduce.3.cloned.1.call-start
  7.2 1.1 fusion.11
  8.4 15.7 %collective-permute-start = (bf16[256,256]{1,0:T(8,128)(2,1)S(1)}, bf16[256,256]{1,0:T(8,128)(2,1)S(1)}, u32[]{:S(2)}, u32[]{:S(2)}) collective-permute-start(bf16[256,256]{1,0:T(8,128)(2,1)S(1)} %get-tuple-element.35), channel_id=1, source_target_pairs={{0,1},{1,2},{2,3},{3,4},{4,5},{5,6},{6,7},{7,0},{8,9},{9,10},{10,1... | collective-permute-start | bytes 393224 | tf_op jit(solution)/shard_map/ppermute | solution.py:13
  24.1 4.4 collective-permute-start.2
  28.5 0.7 compare_select_fusion
  29.2 0.1 copy.15
  29.3 0.1 reshape.133
  29.3 0.7 iota_compare_fusion
  30.1 0.2 collective-permute-done
  30.3 1.9 collective-permute-start.1
  32.3 0.1 copy.14
  32.3 0.1 reshape.138
  32.4 19.6 %collective-permute-done.2 = bf16[256,256]{1,0:T(8,128)(2,1)S(1)} collective-permute-done((bf16[256,256]{1,0:T(8,128)(2,1)S(1)}, bf16[256,256]{1,0:T(8,128)(2,1)S(1)}, u32[]{:S(2)}, u32[]{:S(2)}) %collective-permute-start.2) | collective-permute-done | bytes 131104 | tf_op jit(solution)/shard_map/ppermute | solution.py:13
  52.0 1.9 collective-permute-start.3
  54.0 0.0 collective-permute-done.1
  54.0 2.5 collective-permute-done.3
  56.5 0.1 pad_maximum_fusion
  56.6 2.3 gather_fusion
  58.9 2.4 bitcast_convert_fusion
  61.3 0.0 copy-start.6
  61.3 1.8 convert_reduce_fusion
  63.1 0.9 copy-done.2
  64.0 0.4 convolution_convert_fusion
  64.4 3.1 broadcast_select_fusion
  67.5 6.1 copy.17
  73.6 0.2 broadcast_in_dim.36
  73.8 8.8 scatter_fusion
  82.7 0.8 fusion.10
  83.5 8.7 collective-permute-start.4
  92.2 7.9 collective-permute-start.6
  100.2 2.5 fusion.12
  102.6 0.0 all-reduce.3.cloned.1.call-update
  102.7 0.0 all-reduce.5.cloned.1.call-start
  102.7 28.1 %collective-permute-done.4 = f32[2,128,256]{2,1,0:T(8,128)} collective-permute-done((f32[2,128,256]{2,1,0:T(8,128)}, f32[2,128,256]{2,1,0:T(8,128)}, u32[]{:S(2)}, u32[]{:S(2)}) %collective-permute-start.4) | collective-permute-done | bytes 262176 | tf_op jit(solution)/shard_map/ppermute | solution.py:13
  130.8 1.9 collective-permute-start.5
  132.8 200.3 %psum.30 = f32[256]{0:T(256)S(1)} all-reduce(f32[256]{0:T(256)S(1)} %get-tuple-element.28), channel_id=1, replica_groups=mesh['rows'=64,'cols'=8] {'rows'}, use_global_device_ids=true, to_apply=%region_4.5 | all-reduce | flops 256 | bytes 2048 | tf_op jit(solution)/shard_map/psum | solution.py:76
  333.0 42.3 %psum.31 = f32[256]{0:T(256)S(1)} all-reduce(f32[256]{0:T(256)S(1)} %psum.30), channel_id=1, replica_groups=mesh['rows'=64,'cols'=8] {'cols'}, use_global_device_ids=true, to_apply=%region_5.6 | all-reduce | flops 256 | bytes 2048 | tf_op jit(solution)/shard_map/psum | solution.py:76
  375.4 1.9 collective-permute-start.7
  377.3 0.6 broadcast_multiply_fusion.1
  377.8 1.3 slice.73
  379.2 477.6 %all-reduce.3.cloned.1.call-done = f32[256,256]{1,0:T(8,128)} async-done(((f32[256,256]{1,0:T(8,128)}), f32[256,256]{1,0:T(8,128)}) %all-reduce.3.cloned.1.call-update) | async-done | bytes 262160 | tf_op jit(solution)/shard_map/psum | solution.py:76
  856.8 0.0 all-reduce.5.cloned.1.call-update
  856.9 1.7 fusion.7
  858.6 1.7 fusion.6
  860.3 2.4 convert_element_type.37
  862.7 183.8 %all-reduce.5.cloned.1.call-done = f32[256,256]{1,0:T(8,128)} async-done(((f32[256,256]{1,0:T(8,128)}), f32[256,256]{1,0:T(8,128)}) %all-reduce.5.cloned.1.call-update) | async-done | bytes 262160 | tf_op jit(solution)/shard_map/psum | solution.py:76
  1046.5 1.7 broadcast_multiply_fusion
  (19 shorter events, 0.1 us)
Async XLA Ops:
  7.2 51.7 %copy-start = (bf16[12,3,128,128]{3,2,1,0:T(8,128)(2,1)S(1)}, bf16[12,3,128,128]{3,2,1,0:T(8,128)(2,1)}, u32[]{:S(2)}) copy-start(bf16[12,3,128,128]{3,2,1,0:T(8,128)(2,1)} %param.12) | copy-start | bytes 3538948
  7.2 49.3 %copy-start.1 = (bf16[1536,256]{1,0:T(8,128)(2,1)S(1)}, bf16[1536,256]{1,0:T(8,128)(2,1)}, u32[]{:S(2)}) copy-start(bf16[1536,256]{1,0:T(8,128)(2,1)} %param.11) | copy-start | bytes 2359300
  7.2 849.6 %all-reduce.3.cloned.1.call-start = ((), (), s32[]{:S(2)}) async-start(), calls=%async_computation | async-start | bytes 524288 | tf_op jit(solution)/shard_map/psum | solution.py:76
  8.4 22.0 %collective-permute-start = (bf16[256,256]{1,0:T(8,128)(2,1)S(1)}, bf16[256,256]{1,0:T(8,128)(2,1)S(1)}, u32[]{:S(2)}, u32[]{:S(2)}) collective-permute-start(bf16[256,256]{1,0:T(8,128)(2,1)S(1)} %get-tuple-element.35), channel_id=1, source_target_pairs={{0,1},{1,2},{2,3},{3,4},{4,5},{5,6},{6,7},{7,0},{8,9},{9,10},{10,1... | collective-permute-start | bytes 393224 | tf_op jit(solution)/shard_map/ppermute | solution.py:13
  24.1 28.0 %collective-permute-start.2 = (bf16[256,256]{1,0:T(8,128)(2,1)S(1)}, bf16[256,256]{1,0:T(8,128)(2,1)S(1)}, u32[]{:S(2)}, u32[]{:S(2)}) collective-permute-start(bf16[256,256]{1,0:T(8,128)(2,1)S(1)} %get-tuple-element.36), channel_id=1, source_target_pairs={{0,7},{1,0},{2,1},{3,2},{4,3},{5,4},{6,5},{7,6},{8,15},{9,8},{10,9... | collective-permute-start | bytes 393224 | tf_op jit(solution)/shard_map/ppermute | solution.py:13
  30.3 23.7 %collective-permute-start.1 = (bf16[256,256]{1,0:T(8,128)(2,1)S(1)}, bf16[256,256]{1,0:T(8,128)(2,1)S(1)}, u32[]{:S(2)}, u32[]{:S(2)}) collective-permute-start(bf16[256,256]{1,0:T(8,128)(2,1)S(1)} %collective-permute-done), channel_id=1, source_target_pairs={{0,8},{8,16},{16,24},{24,32},{32,40},{40,48},{48,56},{56,64},{64,7... | collective-permute-start | bytes 393224 | tf_op jit(solution)/shard_map/ppermute | solution.py:19
  52.0 4.4 collective-permute-start.3
  58.9 2.4 copy-start.3
  58.9 2.4 copy-start.4
  58.9 2.4 copy-start.5
  61.3 1.9 copy-start.6
  63.1 0.9 copy-start.2
  83.5 47.3 %collective-permute-start.4 = (f32[2,128,256]{2,1,0:T(8,128)}, f32[2,128,256]{2,1,0:T(8,128)}, u32[]{:S(2)}, u32[]{:S(2)}) collective-permute-start(f32[2,128,256]{2,1,0:T(8,128)} %get-tuple-element.33), channel_id=1, source_target_pairs={{0,1},{1,2},{2,3},{3,4},{4,5},{5,6},{6,7},{7,0},{8,9},{9,10},{10,1... | collective-permute-start | bytes 786440 | tf_op jit(solution)/shard_map/ppermute | solution.py:13
  92.2 283.1 %collective-permute-start.6 = (f32[2,128,256]{2,1,0:T(8,128)}, f32[2,128,256]{2,1,0:T(8,128)S(1)}, u32[]{:S(2)}, u32[]{:S(2)}) collective-permute-start(f32[2,128,256]{2,1,0:T(8,128)} %get-tuple-element.32), channel_id=1, source_target_pairs={{0,7},{1,0},{2,1},{3,2},{4,3},{5,4},{6,5},{7,6},{8,15},{9,8},{10,9... | collective-permute-start | bytes 786440 | tf_op jit(solution)/shard_map/ppermute | solution.py:13
  102.7 943.8 %all-reduce.5.cloned.1.call-start = ((), (), s32[]{:S(2)}) async-start(), calls=%async_computation.1 | async-start | bytes 524288 | tf_op jit(solution)/shard_map/psum | solution.py:76
  130.8 726.0 %collective-permute-start.5 = (f32[2,128,256]{2,1,0:T(8,128)}, f32[2,128,256]{2,1,0:T(8,128)}, u32[]{:S(2)}, u32[]{:S(2)}) collective-permute-start(f32[2,128,256]{2,1,0:T(8,128)} %collective-permute-done.4), channel_id=1, source_target_pairs={{0,8},{8,16},{16,24},{24,32},{32,40},{40,48},{48,56},{56,64},{64,7... | collective-permute-start | bytes 786440 | tf_op jit(solution)/shard_map/ppermute | solution.py:19
  375.4 483.2 %collective-permute-start.7 = (f32[2,128,256]{2,1,0:T(8,128)S(1)}, f32[2,128,256]{2,1,0:T(8,128)}, u32[]{:S(2)}, u32[]{:S(2)}) collective-permute-start(f32[2,128,256]{2,1,0:T(8,128)S(1)} %collective-permute-done.6), channel_id=1, source_target_pairs={{8,0},{16,8},{24,16},{32,24},{40,32},{48,40},{56,48},{64,56},{72,6... | collective-permute-start | bytes 786440 | tf_op jit(solution)/shard_map/ppermute | solution.py:19
Sparse Core Ops, SparseCore 0:
  102.8 754.0 all-reduce.2
  860.0 186.4 all-reduce.4
